TPU v7x, 256 devices: a whole 4x4x8 slice. The times are simulated.
256 devices in a mesh: blk: 16 (over y, x_lo, core), rep: 16 (over z, x_hi).
Axes of the slice: x: 4 (x_hi: 2, x_lo: 2; x = x_hi * 2 + x_lo), y: 4, z: 8, core: 2. Of those that a mesh axis runs over, the one named last changes fastest.
Arguments:
- features: bfloat16 [65536, 128], P(('blk', 'rep')), may hold values from -6 to 6
- edge_rows: int32 [16, 16, 32, 256], P('blk', None, 'rep'), may hold values from 0 to 4095
- edge_cols: int32 [16, 16, 32, 256], P('blk', None, 'rep'), may hold values from 0 to 127
- weight: bfloat16 [128, 256], replicated, may hold values from -0.5 to 0.5
- bias: float32 [256], replicated, may hold values from -3 to 3
- upstream: bfloat16 [65536, 256], P('blk'), may hold values from -6 to 6
- train_mask: int32 [65536], P('blk'), may hold values 0 or 1
Outputs:
- activations: bfloat16 [65536, 256], P(('blk', 'rep'))
- grad_features: bfloat16 [65536, 128], P(('blk', 'rep'))
- grad_weight: float32 [128, 256], replicated
- grad_bias: float32 [256], replicated
Inputs may be any that keep to these rules, and one draw needn't show every extreme that they name: `edge_rows`: target indices within a panel. `edge_cols`: source indices within a column block.
All inputs are finite; a program needn't handle non-finite values. No bound on the sum of `train_mask` on one device may be relied on, other than what follows from the above.
Results may differ from a plain program's by a relative error of at most 0.018.
Values may be sent and summed in bfloat16 or wider, within the bound.
No kernel may reach another device: no remote copies, remote signals or barrier semaphores. Data moves between devices by JAX's collectives and lax.ppermute only.
A program may use at most 64 MiB of HBM per device.

v0:
```python
import math
import jax
import jax.numpy as jnp
from jax import lax
from jax.sharding import PartitionSpec as P

CB = 128


def from_everyone(value, axis):
    copies = jnp.broadcast_to(value, (lax.axis_size(axis), *value.shape))
    return lax.all_to_all(copies, axis, split_axis=0, concat_axis=0, tiled=True)


def in_order(parts, dim):
    lengths = list(parts.shape[1:])
    lengths[dim] *= parts.shape[0]
    return jnp.moveaxis(parts, 0, dim).reshape(lengths)


def gathered_copies(value, axis, dim):
    parts = from_everyone(value, axis)
    return in_order(parts, dim)


def in_blocks(value, dim, count):
    lengths = value.shape
    parts = value.reshape(*lengths[:dim], count, lengths[dim] // count, *lengths[dim + 1 :])
    return jnp.moveaxis(parts, dim, 0)


def summed_on_arrival(value, axis, dim):
    parts = in_blocks(value, dim, lax.axis_size(axis))
    arrived = lax.all_to_all(parts, axis, split_axis=0, concat_axis=0, tiled=True)
    return arrived.astype(jnp.float32).sum(axis=0)


def sent_together(arrays, axis, dim, along):
    widths = [math.prod(a.shape[along:]) for a in arrays]
    both = jnp.concatenate(
        [a.reshape(*a.shape[:along], w) for a, w in zip(arrays, widths)], axis=along
    )
    whole = summed_on_arrival(both, axis, dim)
    parts = jnp.split(whole, [sum(widths[:k]) for k in range(1, len(widths))], axis=along)
    return tuple((b.reshape(*whole.shape[:along], *a.shape[along:]) for a, b in zip(arrays, parts)))


def together(arrays, axis):
    ends = [0]
    for a in arrays:
        ends.append(ends[-1] + a.size)
    subtotal = lax.psum(jnp.concatenate([a.ravel() for a in arrays]), axis)
    return tuple((subtotal[b:e].reshape(a.shape) for a, b, e in zip(arrays, ends, ends[1:])))


def dense_layer(feats, gathered, counts, upstream, train_mask, weight, bias):
    degree = 1.0 + counts
    mixed_in = ((feats.astype(jnp.float32) + gathered) / degree[:, None]).astype(jnp.bfloat16)
    pre_act = jnp.dot(mixed_in, weight, preferred_element_type=jnp.float32) + bias
    gate_value = jax.nn.sigmoid(pre_act)
    activations = (pre_act * gate_value).astype(jnp.bfloat16)
    slope = gate_value * (1.0 + pre_act * (1.0 - gate_value))
    grad_pre = (
        upstream.astype(jnp.float32) * train_mask.astype(jnp.float32)[:, None] * slope
    ).astype(jnp.bfloat16)
    scaled_back = (
        jnp.dot(grad_pre, weight.T, preferred_element_type=jnp.float32) / degree[:, None]
    ).astype(jnp.bfloat16)
    return (mixed_in, activations, grad_pre, scaled_back)


def on_device(features, edge_rows, edge_cols, weight, bias, upstream, train_mask):
    piece_rows, feature_width = features.shape
    edge_slots = edge_rows.shape[-1]
    panel_rows = upstream.shape[0]
    flat_rows = edge_rows.reshape(-1, edge_slots)
    flat_cols = edge_cols.reshape(-1, edge_slots)
    rep_index = lax.axis_index("rep")
    counts_part = jnp.zeros((panel_rows,), jnp.float32).at[flat_rows.reshape(-1)].add(1.0)
    shard_rows = gathered_copies(features, "blk", 0)
    block_count = shard_rows.shape[0] // CB
    targets = flat_rows
    columns = flat_cols
    offsets = (jnp.arange(block_count, dtype=jnp.int32) * CB)[:, None]
    values = jnp.take(shard_rows, (offsets + columns).reshape(-1), axis=0).astype(jnp.float32)
    partial_sums = (
        jnp.zeros((panel_rows, feature_width), jnp.float32).at[targets.reshape(-1)].add(values)
    )
    gathered, counts = sent_together(
        (partial_sums.astype(jnp.bfloat16), counts_part.astype(jnp.bfloat16)), "rep", 0, 1
    )
    own_upstream = lax.dynamic_slice_in_dim(upstream, rep_index * piece_rows, piece_rows, 0)
    own_mask = lax.dynamic_slice_in_dim(train_mask, rep_index * piece_rows, piece_rows, 0)
    mixed_own, activations, grad_own, back_own = dense_layer(
        features, gathered, counts, own_upstream, own_mask, weight, bias
    )
    back_panel = gathered_copies(back_own, "rep", 0)
    weight_part = lax.dot_general(
        mixed_own, grad_own, (((0,), (0,)), ((), ())), preferred_element_type=jnp.float32
    )
    bias_part = jnp.sum(grad_own.astype(jnp.float32), axis=0)
    grad_weight, grad_bias = together((weight_part, bias_part), ("blk", "rep"))
    row_count = piece_rows * lax.axis_size("blk")
    block_count = row_count // CB
    targets = flat_rows
    columns = flat_cols
    values = jnp.take(back_panel, targets.reshape(-1), axis=0).reshape(
        block_count, edge_slots, feature_width
    )
    one_hot = (columns[:, :, None] == jnp.arange(CB, dtype=jnp.int32)[None, None, :]).astype(
        jnp.bfloat16
    )
    block_terms = jnp.einsum("nec,ned->ncd", one_hot, values, preferred_element_type=jnp.float32)
    received = summed_on_arrival(
        block_terms.reshape(row_count, feature_width).astype(jnp.bfloat16), "blk", 0
    )
    grad_features = (back_own.astype(jnp.float32) + received).astype(jnp.bfloat16)
    return (activations, grad_features, grad_weight, grad_bias)


def solution(mesh):
    return jax.shard_map(
        on_device,
        mesh=mesh,
        in_specs=(
            P(("blk", "rep"), None),
            P("blk", None, "rep", None),
            P("blk", None, "rep", None),
            P(),
            P(),
            P("blk", None),
            P("blk"),
        ),
        out_specs=(P(("blk", "rep"), None), P(("blk", "rep"), None), P(), P()),
        check_vma=False,
    )
```

profile of v0, /device:TPU:1, one launch (start us, length us, event | category | flops | bytes accessed | tf_op | source)
XLA Modules:
  0.0 513.4 jit_solution(3568390661544370196)
XLA Ops:
  7.2 0.0 copy-start
  7.2 0.0 copy-start.4
  7.2 0.0 copy-start.3
  7.2 2.1 broadcast_in_dim.33
  9.3 6.9 %all-to-all-start = ((bf16[16,256,128]{2,1,0:T(8,128)(2,1)}), bf16[16,256,128]{2,1,0:T(8,128)(2,1)S(1)}, u32[]{:S(2)}, u32[]{:S(2)}) async-start(bf16[16,256,128]{2,1,0:T(8,128)(2,1)} %broadcast_in_dim.33), calls=%async_computation | async-start | bytes 2097152 | tf_op jit(solution)/shard_map/all_to_all | solution.py:12
  16.2 0.0 copy-done.4
  16.2 0.1 reshape_reshape.7
  16.3 0.1 broadcast_bitcast_fusion
  16.4 0.0 copy-done.3
  16.5 43.2 %scatter_custom_fusion.1 = f32[4096]{0:T(1024)S(1)} fusion(s32[8192]{0:T(1024)S(1)} %bitcast.37, f32[8192]{0:T(1024)S(1)} %broadcast.37, f32[]{:T(128)} %constant.15.clone.1), kind=kCustom, calls=%fused_computation.37 | custom fusion | flops 8192 | bytes 16388 | tf_op jit(solution)/shard_map/scatter-add | solution.py:79
  59.7 3.1 concatenate.15
  62.9 0.0 all-to-all-done
  62.9 73.9 %scatter_custom_fusion = f32[4096,128]{1,0:T(8,128)S(1)} fusion(s32[8192]{0:T(1024)S(1)} %bitcast.38, pred[8192]{0:T(1024)(128)(4,1)S(1)} %compare_and_fusion.1, bf16[]{:T(256)} %constant.11.clone.2, f32[]{:T(128)} %constant.15.clone.1, bf16[4096,128]{1,0:T(8,128)(2,1)S(1)} %bitcast.25, s32[8192]{0:T(1024)S(1)} %broadcast_clamp_fusion), kind=kCustom, calls=%fused_computation.5 | custom fusion | flops 3145728 | bytes 3186694 | tf_op jit(solution)/shard_map/scatter-add | solution.py:87
  136.7 0.0 copy-start.1
  136.8 0.1 convert_element_type.55
  136.9 1.1 copy-done.1
  138.0 0.5 pad_maximum_fusion
  138.4 2.2 copy.16
  140.6 10.6 %all-to-all-start.1 = ((bf16[16,256,129]{1,2,0:T(8,128)(2,1)}), bf16[16,256,129]{1,2,0:T(8,128)(2,1)S(1)}, u32[]{:S(2)}, u32[]{:S(2)}) async-start(bf16[16,256,129]{1,2,0:T(8,128)(2,1)} %copy.16), calls=%async_computation.1 | async-start | bytes 2228224 | tf_op jit(solution)/shard_map/all_to_all | solution.py:34
  151.2 0.8 dynamic-slice_convert_fusion
  152.0 27.8 %all-to-all-done.1 = bf16[16,256,129]{1,2,0:T(8,128)(2,1)S(1)} async-done(((bf16[16,256,129]{1,2,0:T(8,128)(2,1)}), bf16[16,256,129]{1,2,0:T(8,128)(2,1)S(1)}, u32[]{:S(2)}, u32[]{:S(2)}) %all-to-all-start.1) | async-done | bytes 1056800 | tf_op jit(solution)/shard_map/all_to_all | solution.py:34
  179.8 0.2 convert_reduce_fusion
  180.0 0.1 copy.18
  180.1 0.1 divide_convert_fusion
  180.2 1.8 convert_reduce_fusion.2
  182.1 0.2 fusion.7
  182.3 1.2 broadcast_in_dim.36
  183.4 6.0 %all-to-all-start.2 = ((bf16[16,256,128]{2,1,0:T(8,128)(2,1)}), bf16[16,256,128]{2,1,0:T(8,128)(2,1)S(1)}, u32[]{:S(2)}, u32[]{:S(2)}) async-start(bf16[16,256,128]{2,1,0:T(8,128)(2,1)} %broadcast_in_dim.36), calls=%async_computation.2 | async-start | bytes 2097152 | tf_op jit(solution)/shard_map/all_to_all | solution.py:12
  189.4 0.6 eq.15
  190.1 25.4 %all-to-all-done.2 = bf16[16,256,128]{2,1,0:T(8,128)(2,1)S(1)} async-done(((bf16[16,256,128]{2,1,0:T(8,128)(2,1)}), bf16[16,256,128]{2,1,0:T(8,128)(2,1)S(1)}, u32[]{:S(2)}, u32[]{:S(2)}) %all-to-all-start.2) | async-done | bytes 1048608 | tf_op jit(solution)/shard_map/all_to_all | solution.py:12
  215.5 24.0 %gather_fusion = bf16[8192,128]{1,0:T(8,128)(2,1)S(1)} fusion(bf16[4096,128]{1,0:T(8,128)(2,1)S(1)} %bitcast.24, s32[8192]{0:T(1024)S(1)} %fusion.10), kind=kCustom, calls=%fused_computation.1.clone | custom fusion | bytes 4227072 | tf_op jit(solution)/shard_map/jit(_take)/gather | solution.py:107
  239.5 0.0 copy-start.5
  239.5 4.3 broadcast_select_fusion
  243.8 0.0 copy-done.5
  243.8 1.9 fusion.6
  245.7 9.6 %all-to-all-start.3 = ((bf16[16,256,128]{2,1,0:T(8,128)(2,1)}), bf16[16,256,128]{2,1,0:T(8,128)(2,1)S(1)}, u32[]{:S(2)}, u32[]{:S(2)}) async-start(bf16[16,256,128]{2,1,0:T(8,128)(2,1)} %bitcast.6), calls=%async_computation.3 | async-start | bytes 2097152 | tf_op jit(solution)/shard_map/all_to_all | solution.py:34
  255.3 0.0 all-reduce.2.cloned.1.call-start
  255.3 0.2 convolution_bitcast_fusion
  255.5 0.1 copy.22
  255.6 0.7 pad_maximum_fusion.1
  256.3 0.0 all-reduce.2.cloned.1.call-update
  256.3 246.6 %all-reduce.2.cloned.1.call-done = f32[33024]{0:T(1024)} async-done(((f32[33024]{0:T(1024)}), f32[33024]{0:T(1024)}) %all-reduce.2.cloned.1.call-update) | async-done | bytes 132112 | tf_op jit(solution)/shard_map/psum | solution.py:52
  502.9 0.9 slice.23
  503.8 0.7 slice.17
  504.5 1.2 slice.24
  505.8 0.0 all-to-all-done.3
  505.8 0.1 convert_reduce_fusion.1
  505.9 0.6 add_convert_fusion
  (18 shorter events, 0.2 us)
Async XLA Ops:
  7.2 173.1 %copy-start = (bf16[128,256]{1,0:T(8,128)(2,1)S(1)}, bf16[128,256]{1,0:T(8,128)(2,1)}, u32[]{:S(2)}) copy-start(bf16[128,256]{1,0:T(8,128)(2,1)} %param.12) | copy-start | bytes 196612
  7.2 9.0 %copy-start.4 = (s32[1,16,2,256]{3,2,1,0:T(2,128)S(1)}, s32[1,16,2,256]{3,2,1,0:T(2,128)}, u32[]{:S(2)}) copy-start(s32[1,16,2,256]{3,2,1,0:T(2,128)} %param.10) | copy-start | bytes 98308
  7.2 9.2 %copy-start.3 = (s32[1,16,2,256]{3,2,1,0:T(2,128)S(1)}, s32[1,16,2,256]{3,2,1,0:T(2,128)}, u32[]{:S(2)}) copy-start(s32[1,16,2,256]{3,2,1,0:T(2,128)} %param.11) | copy-start | bytes 98308
  9.3 53.6 %all-to-all-start = ((bf16[16,256,128]{2,1,0:T(8,128)(2,1)}), bf16[16,256,128]{2,1,0:T(8,128)(2,1)S(1)}, u32[]{:S(2)}, u32[]{:S(2)}) async-start(bf16[16,256,128]{2,1,0:T(8,128)(2,1)} %broadcast_in_dim.33), calls=%async_computation | async-start | bytes 2097152 | tf_op jit(solution)/shard_map/all_to_all | solution.py:12
  136.7 1.2 copy-start.1
  140.6 39.5 %copy-start.2 = (bf16[256,128]{1,0:T(8,128)(2,1)S(1)}, bf16[256,128]{1,0:T(8,128)(2,1)}, u32[]{:S(2)}) copy-start(bf16[256,128]{1,0:T(8,128)(2,1)} %param.9) | copy-start | bytes 196612
  140.6 39.6 %copy-start.6 = (f32[256]{0:T(256)S(1)}, f32[256]{0:T(256)}, u32[]{:S(2)}) copy-start(f32[256]{0:T(256)} %param.13) | copy-start | bytes 3076
  140.6 39.2 %all-to-all-start.1 = ((bf16[16,256,129]{1,2,0:T(8,128)(2,1)}), bf16[16,256,129]{1,2,0:T(8,128)(2,1)S(1)}, u32[]{:S(2)}, u32[]{:S(2)}) async-start(bf16[16,256,129]{1,2,0:T(8,128)(2,1)} %copy.16), calls=%async_computation.1 | async-start | bytes 2228224 | tf_op jit(solution)/shard_map/all_to_all | solution.py:34
  183.4 32.0 %all-to-all-start.2 = ((bf16[16,256,128]{2,1,0:T(8,128)(2,1)}), bf16[16,256,128]{2,1,0:T(8,128)(2,1)S(1)}, u32[]{:S(2)}, u32[]{:S(2)}) async-start(bf16[16,256,128]{2,1,0:T(8,128)(2,1)} %broadcast_in_dim.36), calls=%async_computation.2 | async-start | bytes 2097152 | tf_op jit(solution)/shard_map/all_to_all | solution.py:12
  239.5 4.3 copy-start.5
  245.7 260.1 %all-to-all-start.3 = ((bf16[16,256,128]{2,1,0:T(8,128)(2,1)}), bf16[16,256,128]{2,1,0:T(8,128)(2,1)S(1)}, u32[]{:S(2)}, u32[]{:S(2)}) async-start(bf16[16,256,128]{2,1,0:T(8,128)(2,1)} %bitcast.6), calls=%async_computation.3 | async-start | bytes 2097152 | tf_op jit(solution)/shard_map/all_to_all | solution.py:34
  255.3 247.6 %all-reduce.2.cloned.1.call-start = ((), (), s32[]{:S(2)}) async-start(), calls=%async_computation.4 | async-start | bytes 270336 | tf_op jit(solution)/shard_map/psum | solution.py:52
Sparse Core Ops, SparseCore 0:
  261.6 241.2 all-reduce.1
where the time goes:
time: 514 us; the launch traced here: 513 us
  waiting for transfers between devices  300 us (58%)
  other arithmetic  124 us (24%)
  local copies, waits for them, and re-layouts  37.6 us (7%)
  starting transfers between devices  33.1 us (6%)
  between operations  14.3 us (3%)
    psum x1, waiting for transfers between devices, together(): subtotal = lax.psum(jnp.concatenate([a.ravel() for a in arrays]), axis)  247 us
    scatter-add x1, other arithmetic, on_device(): jnp.zeros((panel_rows, feature_width), jnp.float32).at[targets.reshape(-1)]  73.9 us
    scatter-add x1, other arithmetic, on_device(): jnp.zeros((panel_rows,), jnp.float32).at[flat_rows.reshape(-1)].add(1.0)  43.2 us
    all_to_all x2, waiting for transfers between devices, summed_on_arrival(): lax.all_to_all(parts, axis, split_axis=0, concat_axis=0, tiled=True)  27.8 us
    all_to_all x2, waiting for transfers between devices, from_everyone(): return lax.all_to_all(copies, axis, split_axis=0, concat_axis=0, tiled=True)  25.4 us
    gather x1, local copies, waits for them, and re-layouts, on_device(): jnp.take(back_panel, targets.reshape(-1), axis=0)  24 us
    all_to_all x2, starting transfers between devices, summed_on_arrival(): lax.all_to_all(parts, axis, split_axis=0, concat_axis=0, tiled=True)  20.2 us
    all_to_all x2, starting transfers between devices, from_everyone(): return lax.all_to_all(copies, axis, split_axis=0, concat_axis=0, tiled=True)  12.9 us
  transfers between devices with their start and end apart: 5, of which 3 were waited for; matrix products, arithmetic and copies ran while one was open for 10% of the time, Pallas kernels for 0%

commit v1 on v0

--- a/solution.py
+++ b/solution.py
@@ -49,7 +49,7 @@
     ends = [0]
     for a in arrays:
         ends.append(ends[-1] + a.size)
-    subtotal = lax.psum(jnp.concatenate([a.ravel() for a in arrays]), axis)
+    subtotal = jnp.sum(lax.all_gather(jnp.concatenate([a.ravel() for a in arrays]), axis), axis=0)
     return tuple((subtotal[b:e].reshape(a.shape) for a, b, e in zip(arrays, ends, ends[1:])))
 
 

time: 514 us -> 994 us (1.93)
  waiting for transfers between devices: 300 us -> 723 us
  other arithmetic: 124 us -> 161 us
  blocking collectives: 0 us -> 27.6 us
    all_gather x0 -> x1, waiting for transfers between devices: none -> 669 us  [together(): lax.all_gather(jnp.concatenate([a.ravel() for a in arrays]), axis)]
    psum x1 -> x0, waiting for transfers between devices: 247 us -> none  [together(): subtotal = lax.psum(jnp.concatenate([a.ravel() for a in arrays]), axis)]
    reduce_sum x0 -> x1, other arithmetic: none -> 37.5 us  [together(): jnp.sum(lax.all_gather(jnp.concatenate([a.ravel() for a in arrays]), axis...]
    all_to_all x0 -> x1, blocking collectives: none -> 27.6 us  [summed_on_arrival(): lax.all_to_all(parts, axis, split_axis=0, concat_axis=0, tiled=True)]
    all_to_all x2 -> x1, starting transfers between devices: 20.2 us -> 10.6 us  [summed_on_arrival(): lax.all_to_all(parts, axis, split_axis=0, concat_axis=0, tiled=True)]
    all_to_all x2 -> x1, waiting for transfers between devices: 27.8 us -> 27.8 us  [summed_on_arrival(): lax.all_to_all(parts, axis, split_axis=0, concat_axis=0, tiled=True)]
  transfers between devices with their start and end apart: 5 -> 4, of which waited for: 3 -> 3; matrix products, arithmetic and copies ran while one was open for 10% -> 8% of each run, Pallas kernels for 0% -> 0%
where the time goes in v1:
time: 994 us; the launch traced here: 988 us
  waiting for transfers between devices  723 us (73%)
  other arithmetic  161 us (16%)
  local copies, waits for them, and re-layouts  36.1 us (4%)
  blocking collectives  27.6 us (3%)
  starting transfers between devices  23.5 us (2%)
  between operations  14.3 us (1%)
    all_gather x1, waiting for transfers between devices, together(): lax.all_gather(jnp.concatenate([a.ravel() for a in arrays]), axis)  669 us
    scatter-add x1, other arithmetic, on_device(): jnp.zeros((panel_rows, feature_width), jnp.float32).at[targets.reshape(-1)]  73.9 us
    scatter-add x1, other arithmetic, on_device(): jnp.zeros((panel_rows,), jnp.float32).at[flat_rows.reshape(-1)].add(1.0)  43.2 us
    reduce_sum x1, other arithmetic, together(): jnp.sum(lax.all_gather(jnp.concatenate([a.ravel() for a in arrays]), axis...  37.5 us
    all_to_all x1, waiting for transfers between devices, summed_on_arrival(): lax.all_to_all(parts, axis, split_axis=0, concat_axis=0, tiled=True)  27.8 us
    all_to_all x1, blocking collectives, summed_on_arrival(): lax.all_to_all(parts, axis, split_axis=0, concat_axis=0, tiled=True)  27.6 us
    all_to_all x2, waiting for transfers between devices, from_everyone(): return lax.all_to_all(copies, axis, split_axis=0, concat_axis=0, tiled=True)  26 us
    gather x1, local copies, waits for them, and re-layouts, on_device(): jnp.take(back_panel, targets.reshape(-1), axis=0)  24 us
  transfers between devices with their start and end apart: 4, of which 3 were waited for; matrix products, arithmetic and copies ran while one was open for 8% of the time, Pallas kernels for 0%

profile of v1, /device:TPU:1, one launch (start us, length us, event | category | flops | bytes accessed | tf_op | source)
XLA Modules:
  0.0 988.5 jit_solution(3612779532602914927)
XLA Ops:
  7.2 0.0 copy-start
  7.2 0.0 copy-start.4
  7.2 0.0 copy-start.3
  7.2 2.1 broadcast_in_dim.33
  9.3 6.9 all-to-all-start
  16.2 0.0 copy-done.4
  16.2 0.1 reshape_reshape.7
  16.3 43.2 %scatter_custom_fusion.1 = f32[4096]{0:T(1024)S(1)} fusion(s32[8192]{0:T(1024)S(1)} %bitcast.38, f32[8192]{0:T(1024)S(1)} %broadcast.37, f32[]{:T(128)} %constant.15.clone.1), kind=kCustom, calls=%fused_computation.37 | custom fusion | flops 8192 | bytes 16388 | tf_op jit(solution)/shard_map/scatter-add | solution.py:79
  59.6 3.1 concatenate.15
  62.7 0.1 broadcast_bitcast_fusion
  62.8 0.0 copy-done.3
  62.9 0.0 all-to-all-done
  62.9 73.9 %scatter_custom_fusion = f32[4096,128]{1,0:T(8,128)S(1)} fusion(s32[8192]{0:T(1024)S(1)} %bitcast.39, pred[8192]{0:T(1024)(128)(4,1)S(1)} %compare_and_fusion.1, bf16[]{:T(256)} %constant.11.clone.2, f32[]{:T(128)} %constant.15.clone.1, bf16[4096,128]{1,0:T(8,128)(2,1)S(1)} %bitcast.25, s32[8192]{0:T(1024)S(1)} %broadcast_clamp_fusion), kind=kCustom, calls=%fused_computation.5 | custom fusion | flops 3145728 | bytes 3186694 | tf_op jit(solution)/shard_map/scatter-add | solution.py:87
  136.8 0.0 copy-start.1
  136.8 0.1 convert_element_type.55
  136.9 1.1 copy-done.1
  138.0 0.5 pad_maximum_fusion
  138.5 2.1 copy.16
  140.6 0.0 copy-start.2
  140.6 10.6 %all-to-all-start.1 = ((bf16[16,256,129]{1,2,0:T(8,128)(2,1)}), bf16[16,256,129]{1,2,0:T(8,128)(2,1)S(1)}, u32[]{:S(2)}, u32[]{:S(2)}) async-start(bf16[16,256,129]{1,2,0:T(8,128)(2,1)} %copy.16), calls=%async_computation.1 | async-start | bytes 2228224 | tf_op jit(solution)/shard_map/all_to_all | solution.py:34
  151.2 0.0 all-gather.4.cloned.1.call-start
  151.2 0.8 dynamic-slice_convert_fusion
  152.0 27.8 %all-to-all-done.1 = bf16[16,256,129]{1,2,0:T(8,128)(2,1)S(1)} async-done(((bf16[16,256,129]{1,2,0:T(8,128)(2,1)}), bf16[16,256,129]{1,2,0:T(8,128)(2,1)S(1)}, u32[]{:S(2)}, u32[]{:S(2)}) %all-to-all-start.1) | async-done | bytes 1056800 | tf_op jit(solution)/shard_map/all_to_all | solution.py:34
  179.8 0.2 convert_reduce_fusion
  180.0 0.1 copy.18
  180.1 0.0 copy-done.2
  180.1 0.1 divide_convert_fusion
  180.2 0.0 copy-done
  180.2 0.0 copy-done.5
  180.2 1.8 convert_reduce_fusion.2
  182.1 0.2 convolution_bitcast_fusion
  182.3 0.1 copy.22
  182.4 0.8 reshape.125
  183.1 0.0 all-gather.4.cloned.1.call-update
  183.1 0.2 fusion.7
  183.3 1.2 broadcast_in_dim.36
  184.5 6.0 all-to-all-start.2
  190.6 26.0 %all-to-all-done.2 = bf16[16,256,128]{2,1,0:T(8,128)(2,1)S(1)} async-done(((bf16[16,256,128]{2,1,0:T(8,128)(2,1)}), bf16[16,256,128]{2,1,0:T(8,128)(2,1)S(1)}, u32[]{:S(2)}, u32[]{:S(2)}) %all-to-all-start.2) | async-done | bytes 1048608 | tf_op jit(solution)/shard_map/all_to_all | solution.py:12
  216.6 24.0 %gather_fusion = bf16[8192,128]{1,0:T(8,128)(2,1)S(1)} fusion(bf16[4096,128]{1,0:T(8,128)(2,1)S(1)} %bitcast.24, s32[8192]{0:T(1024)S(1)} %fusion.10), kind=kCustom, calls=%fused_computation.1.clone | custom fusion | bytes 4227072 | tf_op jit(solution)/shard_map/jit(_take)/gather | solution.py:107
  240.6 4.3 broadcast_select_fusion
  244.9 0.9 fusion.6
  245.8 27.6 %all_to_all.20 = bf16[16,256,128]{2,1,0:T(8,128)(2,1)S(1)} all-to-all(bf16[16,256,128]{2,1,0:T(8,128)(2,1)S(1)} %bitcast.28), channel_id=1, replica_groups=mesh['blk'=16,'rep'=16] {'blk'}, dimensions={0} | all-to-all | bytes 2097152 | tf_op jit(solution)/shard_map/all_to_all | solution.py:34
  273.3 0.1 convert_reduce_fusion.1
  273.5 0.6 add_convert_fusion
  274.1 668.8 %all-gather.4.cloned.1.call-done = f32[256,1,33024]{2,1,0:T(1,128)} async-done(((f32[1,1,33024]{2,1,0:T(1,128)}), f32[256,1,33024]{2,1,0:T(1,128)}) %all-gather.4.cloned.1.call-update) | async-done | bytes 33816592 | tf_op jit(solution)/shard_map/all_gather | solution.py:52
  942.9 37.5 %reduce_sum.39 = f32[33024]{0:T(1024)S(1)} reduce(f32[256,1,33024]{2,1,0:T(1,128)} %all-gather.4.cloned.1.call-done, f32[]{:T(128)} %constant.15.clone.1), dimensions={0,1}, to_apply=%region_5.7 | reduce | flops 8421120 | bytes 33948676 | tf_op jit(solution)/shard_map/reduce_sum | solution.py:52
  980.4 0.6 slice.24
  980.9 0.7 slice.17
  (17 shorter events, 0.2 us)
Async XLA Ops:
  7.2 173.1 %copy-start = (bf16[128,256]{1,0:T(8,128)(2,1)S(1)}, bf16[128,256]{1,0:T(8,128)(2,1)}, u32[]{:S(2)}) copy-start(bf16[128,256]{1,0:T(8,128)(2,1)} %param.12) | copy-start | bytes 196612
  7.2 9.0 copy-start.4
  7.2 55.6 %copy-start.3 = (s32[1,16,2,256]{3,2,1,0:T(2,128)S(1)}, s32[1,16,2,256]{3,2,1,0:T(2,128)}, u32[]{:S(2)}) copy-start(s32[1,16,2,256]{3,2,1,0:T(2,128)} %param.11) | copy-start | bytes 98308
  9.3 53.6 %all-to-all-start = ((bf16[16,256,128]{2,1,0:T(8,128)(2,1)}), bf16[16,256,128]{2,1,0:T(8,128)(2,1)S(1)}, u32[]{:S(2)}, u32[]{:S(2)}) async-start(bf16[16,256,128]{2,1,0:T(8,128)(2,1)} %broadcast_in_dim.33), calls=%async_computation | async-start | bytes 2097152 | tf_op jit(solution)/shard_map/all_to_all | solution.py:12
  136.8 1.2 copy-start.1
  140.6 39.5 %copy-start.2 = (bf16[256,128]{1,0:T(8,128)(2,1)S(1)}, bf16[256,128]{1,0:T(8,128)(2,1)}, u32[]{:S(2)}) copy-start(bf16[256,128]{1,0:T(8,128)(2,1)} %param.9) | copy-start | bytes 196612
  140.6 39.6 %copy-start.5 = (f32[256]{0:T(256)S(1)}, f32[256]{0:T(256)}, u32[]{:S(2)}) copy-start(f32[256]{0:T(256)} %param.13) | copy-start | bytes 3076
  140.6 39.2 %all-to-all-start.1 = ((bf16[16,256,129]{1,2,0:T(8,128)(2,1)}), bf16[16,256,129]{1,2,0:T(8,128)(2,1)S(1)}, u32[]{:S(2)}, u32[]{:S(2)}) async-start(bf16[16,256,129]{1,2,0:T(8,128)(2,1)} %copy.16), calls=%async_computation.1 | async-start | bytes 2228224 | tf_op jit(solution)/shard_map/all_to_all | solution.py:34
  151.2 791.7 %all-gather.4.cloned.1.call-start = ((), (), s32[]{:S(2)}) async-start(), calls=%async_computation.4 | async-start | bytes 33948672 | tf_op jit(solution)/shard_map/all_gather | solution.py:52
  184.5 32.0 %all-to-all-start.2 = ((bf16[16,256,128]{2,1,0:T(8,128)(2,1)}), bf16[16,256,128]{2,1,0:T(8,128)(2,1)S(1)}, u32[]{:S(2)}, u32[]{:S(2)}) async-start(bf16[16,256,128]{2,1,0:T(8,128)(2,1)} %broadcast_in_dim.36), calls=%async_computation.2 | async-start | bytes 2097152 | tf_op jit(solution)/shard_map/all_to_all | solution.py:12
Sparse Core Ops, SparseCore 0:
  183.3 759.5 all-gather.3
